TPU v7x, 32 devices: a whole 2x2x4 slice. The times are simulated.
32 devices in a mesh: groups: 2 (over x), ctx: 16 (over z, y, core).
Axes of the slice: x: 2, y: 2, z: 4, core: 2. Of those that a mesh axis runs over, the one named last changes fastest.
Arguments:
- queries: bfloat16 [8192, 2560], P(('groups', 'ctx')), parts along dimension 0, may hold values from -6 to 6
- keys: bfloat16 [8192, 2560], P(('groups', 'ctx')), parts along dimension 0, may hold values from -6 to 6
- values: bfloat16 [8192, 2560], P(('groups', 'ctx')), parts along dimension 0, may hold values from -6 to 6
- kv_lists: int32 [16, 4, 2, 8], P('ctx'), may hold values from 0 to 7, as said below
- kv_counts: int32 [16, 4, 2], P('ctx'), may hold values from 0 to 8, as said below
Outputs:
- attended: bfloat16 [8192, 2560], P(('groups', 'ctx')), parts along dimension 0
There are 2 independent parts, one for each index of `groups`. A program takes and returns all parts, laid end to end along the dimension named above; an argument that names none is the same for every part. Nothing has to cross between parts.
Inputs may be any that keep to these rules, and one draw needn't show every extreme that they name: For every device d, level k and side s, the first 8 // 2**k entries of kv_lists[d, k, s] are distinct block indices; later entries are never read. kv_counts[d, k, s] is at most 8 // 2**k and reaches it for some device at every level and side; it is 0 exactly where the partner d - 2**k (s = 0) or d + 2**k (s = 1) lies outside 0 to 15, else 1 or more.
All inputs are finite; a program needn't handle non-finite values.
Results may differ from a plain program's by a relative error of at most 0.005.
Values may be sent and summed in bfloat16 or wider, within the bound.
A program may use at most 128 MiB of HBM per device.

v0:
```python
import functools
import math

import jax
import jax.numpy as jnp
from jax import lax
from jax.experimental import pallas as pl
from jax.experimental.pallas import tpu as pltpu
from jax.sharding import PartitionSpec as P

HEAD = 128
MASKED = -1e30
CHUNKS = 4
MESH = pl.DeviceIdType.MESH


def body(
    n_ctx, nblk,
    q_hbm, k_hbm, v_hbm, lists, counts, out_ref,
    q_ref, k_ref, v_ref,
    near, forwarded, big, inner, outer, far, far_pack, relay_pack, hop, pick_near, pick_far, got_near, got_far,
    acc, top, tot,
    s_list, s_near, s_full, s_far, s_relay, s_fwd, s_pack, s_hop,
    r_list, r_near, r_big, r_far, r_fwd, r_outer, r_hop, r_own,
):
    own = [
        pltpu.make_async_copy(src, dst, r_own.at[i])
        for i, (src, dst) in enumerate(((k_hbm, k_ref), (v_hbm, v_ref), (q_hbm, q_ref)))
    ]
    for copy in own:
        copy.start()
    rows, width = q_ref.shape
    heads = width // HEAD
    bs = rows // nblk
    half = rows // 2
    cap1, cap2, cap3 = nblk // 2, nblk // 4, nblk // 8
    rate = math.log2(math.e) / math.sqrt(HEAD)

    d = lax.axis_index("ctx")
    place = lax.rem(d, 4)
    quad = d // 4
    quads = n_ctx // 4
    left = place < 2
    s = jnp.where(left, 1, -1)
    gate = (place == 1) | (place == 2)
    outermost = jnp.logical_not(gate)
    has_out = jnp.where(left, quad > 0, quad < quads - 1)
    has_in = jnp.where(left, quad < quads - 1, quad > 0)
    side_in = jnp.where(left, 1, 0)
    side_out = 1 - side_in
    twin = jnp.where(gate, d - s, d + s)
    relay_to = d + 3 * s
    relay_from = d - 3 * s
    relays = gate & has_in
    gets_relay = outermost & has_out
    forwards = gate | has_out
    fwd_arrives = outermost | has_out

    fars = []
    for distance in (4, 8):
        fars.append((d + distance, d + distance < n_ctx))
        fars.append((d - distance, d - distance >= 0))

    far_rows = (cap2 * bs, cap2 * bs, cap3 * bs, cap3 * bs)
    far_start = (0, cap2 * bs, 2 * cap2 * bs, (2 * cap2 + cap3) * bs)
    ahead = lax.broadcasted_iota(jnp.int32, (bs, rows), 1) - lax.broadcasted_iota(
        jnp.int32, (bs, rows), 0
    )

    def single_ones(level, side, j):
        hit = ahead == lists[0, level, side, j] * bs
        return jnp.where(hit, 1.0, 0.0).astype(jnp.bfloat16)

    for i in range(4):
        for j in range(far_rows[i] // bs):
            pick_far[pl.ds(far_start[i] + j * bs, bs), :] = single_ones(2 + i // 2, i % 2, j)
    for side in range(2):
        for j in range(cap1):
            pick_near[side, pl.ds(j * bs, bs), :] = single_ones(1, side, j)

    def to(device):
        return {"ctx": device}

    barrier = pltpu.get_barrier_semaphore()
    partners = [(p, ok) for p, ok in fars]
    always = jnp.bool_(True)
    partners += [
        (twin, always),
        (d + s, gate),
        (d + 3 * s, outermost),
        (relay_to, relays),
        (relay_from, gets_relay),
    ]
    count = jnp.int32(0)
    for p, ok in partners:
        count = count + ok.astype(jnp.int32)

        @pl.when(ok)
        def _(p=p):
            pl.semaphore_signal(barrier, inc=1, device_id=to(p), device_id_type=MESH)

    pl.semaphore_wait(barrier, count)

    def remote(src, dst, ssem, rsem, device):
        return pltpu.make_async_remote_copy(
            src_ref=src, dst_ref=dst, send_sem=ssem, recv_sem=rsem,
            device_id=to(device), device_id_type=MESH,
        )

    def pick_copy(i, device):
        if i == 4:
            return remote(pick_near.at[side_out], got_near, s_list.at[4], r_list.at[4], device)
        r = pl.ds(far_start[i], far_rows[i])
        return remote(pick_far.at[r], got_far.at[r], s_list.at[i], r_list.at[i], device)

    flip = (1, 0, 3, 2)
    sends_list = [(flip[i], p, ok) for i, (p, ok) in enumerate(fars)] + [(4, relay_from, gets_relay)]
    has_list = [(i, p, ok) for i, (p, ok) in enumerate(fars)] + [(4, relay_to, relays)]

    step_cols = 4 * HEAD if width % (4 * HEAD) == 0 else HEAD

    def gather(pick, sources, dst_of):
        def go(i, carry):
            cols = pl.ds(pl.multiple_of(i * step_cols, step_cols), step_cols)
            for kv in range(len(sources)):
                rows_got = jnp.dot(pick, sources[kv](cols), preferred_element_type=jnp.float32)
                dst_of(kv, cols, rows_got.astype(jnp.bfloat16))
            return carry

        lax.fori_loop(0, width // step_cols, go, 0)

    def part(c):
        return c // 2, pl.ds((c % 2) * half, half)

    def near_copy(c):
        kv, r = part(c)
        return remote((k_hbm, v_hbm)[kv].at[r], near.at[kv, r], s_near.at[c], r_near.at[c], twin)

    def cross_copy(c):
        kv, r = part(c)
        return remote(
            (k_hbm, v_hbm)[kv].at[r], big.at[0, kv, r], s_full.at[0, c], r_big.at[0, c], d + s
        )

    def twin_copy(c):
        kv, r = part(c)
        return remote(near.at[kv, r], big.at[1, kv, r], s_full.at[1, c], r_big.at[1, c], d + s)

    def relay_copy(c):
        kv, r = part(c)
        return remote(big.at[1, kv, r], big.at[0, kv, r], s_relay.at[c], r_big.at[0, c], relay_to)

    def fwd_copy(c):
        kv, r = part(c)
        return remote(big.at[0, kv, r], forwarded.at[kv, r], s_fwd.at[c], r_fwd.at[c], twin)

    def big_wait(slot, c):
        kv, r = part(c)
        remote(big.at[slot, kv, r], big.at[slot, kv, r], s_relay.at[c], r_big.at[slot, c], twin).wait_recv()

    def far_copy(i):
        r = pl.ds(far_start[i], far_rows[i])
        return remote(far_pack.at[:, r], far.at[:, r], s_far.at[i], r_far.at[i], fars[i][0])

    def pack_copy(kv):
        return remote(relay_pack.at[kv], outer.at[kv], s_pack.at[kv], r_outer.at[kv], relay_to)

    def hop_copy():
        kv, r = part(CHUNKS - 1)
        return remote((k_hbm, v_hbm)[kv].at[r], hop, s_hop.at[0], r_hop, d - 4 * s)

    def hop_on_copy():
        kv, r = part(CHUNKS - 1)
        return remote(hop, big.at[0, kv, r], s_hop.at[1], r_big.at[0, CHUNKS - 1], d + 3 * s)

    for slot, p, ok in sends_list:
        @pl.when(ok)
        def _(slot=slot, p=p):
            pick_copy(slot, p).start()

    for c in range(CHUNKS):
        near_copy(c).start()

    @pl.when(gate)
    def _():
        cross_copy(0).start()

    @pl.when(gets_relay)
    def _():
        hop_copy().start()

    for copy in own:
        copy.wait()

    for slot, p, ok in has_list:
        @pl.when(ok)
        def _(slot=slot, p=p):
            pick_copy(slot, p).wait_recv()
            if slot < 4:
                r = pl.ds(far_start[slot], far_rows[slot])

                def put(kv, cols, x):
                    far_pack[kv, r, cols] = x

                gather(got_far[r, :], (lambda c: k_ref[:, c], lambda c: v_ref[:, c]), put)
                far_copy(slot).start()

    @pl.when(gate)
    def _():
        for c in range(CHUNKS):
            near_copy(c).wait_recv()
        twin_copy(0).start()
        cross_copy(1).start()
        twin_copy(1).start()
        cross_copy(2).start()
        cross_copy(3).start()
        twin_copy(2).start()
        twin_copy(3).start()

    def as_bias(seen):
        return jnp.where(seen, 0.0, MASKED).astype(jnp.float32)

    def full_bias(side):
        block = lax.broadcasted_iota(jnp.int32, (1, rows), 1) // bs
        seen = jnp.zeros((1, rows), jnp.int32)
        for j in range(nblk):
            hit = (block == lists[0, 0, side, j]) & (jnp.full((1, rows), j) < counts[0, side, 0])
            seen = seen + hit.astype(jnp.int32)
        return as_bias(seen > 0)

    def listed_bias(side):
        column = lax.broadcasted_iota(jnp.int32, (1, cap1 * bs), 1)
        return as_bias(column < counts[0, side, 1] * bs)

    def wide(x, n):
        k = n // HEAD
        whole = jnp.concatenate([x] * k, axis=1) if k > 1 else x
        if n % HEAD:
            whole = jnp.concatenate([x] * (k + 1), axis=1)[:, :n]
        return whole

    def folded(p):
        n = p.shape[1]
        total = p[:, :HEAD]
        for i in range(1, n // HEAD):
            total = total + p[:, i * HEAD:(i + 1) * HEAD]
        return total

    together = max(n for n in (1, 2, 3, 4, 5) if heads % n == 0)

    def by_heads(one):
        def step(i, carry):
            for u in range(together):
                one(together * i + u)
            return carry

        lax.fori_loop(0, heads // together, step, 0)

    def attend(keys, values, bias, first=False):
        def one(h):
            cols = pl.ds(pl.multiple_of(h * HEAD, HEAD), HEAD)
            sc = lax.dot_general(
                q_ref[:, cols], keys(cols), (((1,), (1,)), ((), ())),
                preferred_element_type=jnp.float32,
            ) * rate
            if bias is not None:
                sc = sc + bias
            n = sc.shape[1]
            best = jnp.broadcast_to(jnp.max(sc, axis=1, keepdims=True), (rows, HEAD))
            if not first:
                old = top[h]
                best = jnp.maximum(old, best)
            p = jnp.exp2(sc - wide(best, n))
            mixed = jnp.dot(
                p.astype(jnp.bfloat16), values(cols), preferred_element_type=jnp.float32
            )
            part_sum = folded(p)
            if first:
                tot[h] = part_sum
                acc[h] = mixed
            else:
                factor = jnp.exp2(old - best)
                tot[h] = tot[h] * factor + part_sum
                acc[h] = acc[h] * factor + mixed
            top[h] = best

        by_heads(one)

    def put_inner(kv, cols, x):
        inner[kv, :, cols] = x

    def put_outer(kv, cols, x):
        outer[kv, :, cols] = x

    attend(lambda c: k_ref[:, c], lambda c: v_ref[:, c], None, first=True)

    @pl.when(outermost & has_in)
    def _():
        hop_copy().wait_recv()
        hop_on_copy().start()

    @pl.when(outermost)
    def _():
        for c in range(CHUNKS):
            near_copy(c).wait_recv()

    attend(
        lambda c: near[0, :, c], lambda c: near[1, :, c],
        full_bias(jnp.where(gate, side_out, side_in)),
    )

    def pass_cross(c):
        big_wait(0, c)
        fwd_copy(c).start()

    def pass_twin(c):
        big_wait(1, c)

        @pl.when(has_in)
        def _():
            relay_copy(c).start()

    def pass_listed(kv):
        @pl.when(has_in)
        def _():
            def put_relay(_, cols, x):
                relay_pack[kv, :, cols] = x

            gather(got_near[...], (lambda c: big[0, kv, :, c],), put_relay)
            pack_copy(kv).start()

    @pl.when(gate)
    def _():
        pass_twin(0)
        pass_cross(0)
        pass_cross(1)
        pass_listed(0)
        pass_twin(1)

    arrives = [fars[1], fars[0], fars[3], fars[2]]
    for i in range(4):
        @pl.when(arrives[i][1])
        def _(i=i):
            far_copy(i).wait_recv()

        @pl.when(jnp.logical_not(arrives[i][1]))
        def _(i=i):
            for kv in range(2):
                far[kv, pl.ds(far_start[i], far_rows[i]), :] = jnp.zeros(
                    (far_rows[i], width), far.dtype
                )

    spare = (-sum(far_rows)) % HEAD
    if spare:
        for kv in range(2):
            far[kv, pl.ds(sum(far_rows), spare), :] = jnp.zeros((spare, width), far.dtype)
    column = lax.broadcasted_iota(jnp.int32, (1, sum(far_rows) + spare), 1)
    limit = jnp.zeros(column.shape, jnp.int32)
    for i in range(4):
        end = far_start[i] + counts[0, i % 2, 2 + i // 2] * bs
        limit = jnp.where(column >= far_start[i], end, limit)
    limit = jnp.where(column >= sum(far_rows), 0, limit)
    far_bias = as_bias(column < limit)
    attend(lambda c: far[0, :, c], lambda c: far[1, :, c], far_bias)

    def attend_inner():
        attend(lambda c: inner[0, :, c], lambda c: inner[1, :, c], listed_bias(side_in))

    def attend_big():
        attend(
            lambda c: big[0, 0, :, c], lambda c: big[0, 1, :, c],
            full_bias(jnp.where(gate, side_in, side_out)),
        )

    def attend_outer():
        attend(lambda c: outer[0, :, c], lambda c: outer[1, :, c], listed_bias(side_out))

    @pl.when(gate)
    def _():
        pass_cross(2)
        pass_cross(3)
        pass_listed(1)
        attend_big()
        pass_twin(2)
        big_wait(1, 3)
        gather(pick_near[side_in], (lambda c: big[1, 0, :, c], lambda c: big[1, 1, :, c]), put_inner)
        attend_inner()

        @pl.when(has_out)
        def _():
            for c in range(CHUNKS):
                fwd_copy(c).wait_recv()
            gather(
                pick_near[side_out],
                (lambda c: forwarded[0, :, c], lambda c: forwarded[1, :, c]), put_outer,
            )
            attend_outer()

    @pl.when(outermost)
    def _():
        @pl.when(has_out)
        def _():
            for c in (0, 1, 3):
                pass_cross(c)

        for c in range(CHUNKS):
            fwd_copy(c).wait_recv()
        gather(
            pick_near[side_in],
            (lambda c: forwarded[0, :, c], lambda c: forwarded[1, :, c]), put_inner,
        )
        attend_inner()

        @pl.when(has_out)
        def _():
            for kv in range(2):
                pack_copy(kv).wait_recv()
            attend_outer()
            pass_cross(2)
            attend_big()

    def finish(h):
        cols = pl.ds(pl.multiple_of(h * HEAD, HEAD), HEAD)
        total = jnp.sum(tot[h], axis=1, keepdims=True)
        out_ref[:, cols] = (acc[h] / total).astype(out_ref.dtype)

    by_heads(finish)

    for slot, p, ok in sends_list:
        @pl.when(ok)
        def _(slot=slot, p=p):
            pick_copy(slot, p).wait_send()
    for c in range(CHUNKS):
        near_copy(c).wait_send()

    @pl.when(gate)
    def _():
        for c in range(CHUNKS):
            cross_copy(c).wait_send()
            twin_copy(c).wait_send()

    for i, (p, ok) in enumerate(fars):
        @pl.when(ok)
        def _(i=i):
            far_copy(i).wait_send()

    @pl.when(relays)
    def _():
        for c in range(CHUNKS - 1):
            relay_copy(c).wait_send()
        for kv in range(2):
            pack_copy(kv).wait_send()

    @pl.when(gets_relay)
    def _():
        hop_copy().wait_send()

    @pl.when(outermost & has_in)
    def _():
        hop_on_copy().wait_send()

    @pl.when(forwards)
    def _():
        for c in range(CHUNKS):
            fwd_copy(c).wait_send()


def shards(n_ctx, queries, keys, values, kv_lists, kv_counts):
    rows, width = queries.shape
    heads = width // HEAD
    nblk = kv_lists.shape[3]
    bs = rows // nblk
    cap1 = nblk // 2
    far_rows = 2 * (nblk // 4 + nblk // 8) * bs
    far_room = far_rows + (-far_rows) % HEAD
    kv = jnp.bfloat16
    vmem = pl.BlockSpec(memory_space=pltpu.VMEM)
    hbm = pl.BlockSpec(memory_space=pl.ANY)
    smem = pl.BlockSpec(memory_space=pltpu.SMEM)
    dma = pltpu.SemaphoreType.DMA
    return pl.pallas_call(
        functools.partial(body, n_ctx, nblk),
        out_shape=jax.ShapeDtypeStruct((rows, width), jnp.bfloat16),
        in_specs=[hbm, hbm, hbm, smem, smem],
        out_specs=vmem,
        scratch_shapes=[
            pltpu.VMEM((rows, width), kv),
            pltpu.VMEM((rows, width), kv),
            pltpu.VMEM((rows, width), kv),
            pltpu.VMEM((2, rows, width), kv),
            pltpu.VMEM((2, rows, width), kv),
            pltpu.VMEM((2, 2, rows, width), kv),
            pltpu.VMEM((2, cap1 * bs, width), kv),
            pltpu.VMEM((2, cap1 * bs, width), kv),
            pltpu.VMEM((2, far_room, width), kv),
            pltpu.VMEM((2, far_rows, width), kv),
            pltpu.VMEM((2, cap1 * bs, width), kv),
            pltpu.VMEM((rows // 2, width), kv),
            pltpu.VMEM((2, cap1 * bs, rows), kv),
            pltpu.VMEM((far_rows, rows), kv),
            pltpu.VMEM((cap1 * bs, rows), kv),
            pltpu.VMEM((far_rows, rows), kv),
            pltpu.VMEM((heads, rows, HEAD), jnp.float32),
            pltpu.VMEM((heads, rows, HEAD), jnp.float32),
            pltpu.VMEM((heads, rows, HEAD), jnp.float32),
            dma((5,)), dma((CHUNKS,)), dma((2, CHUNKS)), dma((4,)), dma((CHUNKS,)), dma((CHUNKS,)), dma((2,)), dma((2,)),
            dma((5,)), dma((CHUNKS,)), dma((2, CHUNKS)), dma((4,)), dma((CHUNKS,)), dma((2,)), dma, dma((3,)),
        ],
        compiler_params=pltpu.CompilerParams(
            collective_id=0, has_side_effects=True, vmem_limit_bytes=60 * 1024 * 1024
        ),
        name="radial",
    )(queries, keys, values, kv_lists, jnp.swapaxes(kv_counts, 1, 2))


def solution(mesh):
    in_specs = (
        P(("groups", "ctx"), None),
        P(("groups", "ctx"), None),
        P(("groups", "ctx"), None),
        P("ctx", None, None, None),
        P("ctx", None, None),
    )
    out_specs = P(("groups", "ctx"), None)
    return jax.shard_map(
        functools.partial(shards, mesh.shape["ctx"]),
        mesh=mesh, in_specs=in_specs, out_specs=out_specs, check_vma=False,
    )
```

profile of v0, /device:TPU:17, one launch (start us, length us, event | category | flops | bytes accessed | tf_op | source)
XLA Modules:
  0.0 83.9 jit_solution(4143283190705454960)
XLA Ops:
  0.0 81.4 %radial.1 = bf16[256,2560]{1,0:T(8,128)(2,1)} custom-call(bf16[256,2560]{1,0:T(8,128)(2,1)} %q_hbm.1, bf16[256,2560]{1,0:T(8,128)(2,1)} %k_hbm.1, bf16[256,2560]{1,0:T(8,128)(2,1)} %v_hbm.1, s32[1,4,2,8]{3,2,1,0:T(2,128)} %lists.1, s32[1,2,4]{2,1,0:T(2,128)} %bitcast.1), custom_call_target="tpu_custom_call" | custom-call | tf_op jit(solution)/shard_map/radial/pallas_call | solution.py:481
  81.4 2.5 %copy.7 = bf16[256,2560]{1,0:T(8,128)(2,1)} copy(bf16[256,2560]{1,0:T(8,128)(2,1)} %radial.1) | data formatting | bytes 2621440
where the time goes:
time: 84 us; the launch traced here: 83.9 us
  Pallas kernels  81.4 us (97%)
  local copies, waits for them, and re-layouts  2.46 us (3%)
    pallas_call x1, Pallas kernels, shards(): pl.pallas_call(functools.partial(body, n_ctx, nblk), out_shape=jax.ShapeD...  81.4 us
    unnamed x1, local copies, waits for them, and re-layouts  2.46 us

commit v1 on v0

v1 whole, which is shorter than its diff:
```python
import functools
import math

import jax
import jax.numpy as jnp
from jax import lax
from jax.experimental import pallas as pl
from jax.experimental.pallas import tpu as pltpu
from jax.sharding import PartitionSpec as P

HEAD = 128
MASKED = -1e30
PIECE_HEADS = 2
MESH = pl.DeviceIdType.MESH


def body(
    n_ctx, nblk, piece,
    q_hbm, k_hbm, v_hbm, lists, counts, out_ref,
    q_ref, k_ref, v_ref,
    near, across, passed, skew, skew_pack, far, far_pack, stage,
    q_got, o_send, o_got, lse_send, lse_got,
    acc, top, tot, bias_near, bias_late, bias_guest, lists_got, counts_got,
    s_list, s_count, s_near, s_across, s_passed, s_skew, s_far, s_q, s_o, s_lse,
    r_own, r_list, r_count, r_near, r_across, r_passed, r_skew, r_far, r_q, r_o, r_lse,
):
    own = [
        pltpu.make_async_copy(src, dst, r_own.at[i])
        for i, (src, dst) in enumerate(((k_hbm, k_ref), (v_hbm, v_ref), (q_hbm, q_ref)))
    ]
    for copy in own:
        copy.start()
    rows, width = q_ref.shape
    heads = width // HEAD
    bs = rows // nblk
    cap1, cap2, cap3 = nblk // 2, nblk // 4, nblk // 8
    rate = math.log2(math.e) / math.sqrt(HEAD)
    cols_piece = piece * HEAD
    pieces = heads // piece
    far_room = far.shape[1] * bs

    d = lax.axis_index("ctx")
    place = lax.rem(d, 4)
    quad = d // 4
    quads = n_ctx // 4
    left = place < 2
    s = jnp.where(left, 1, -1)
    gate = (place == 1) | (place == 2)
    outer = jnp.logical_not(gate)
    has_out = jnp.where(left, quad > 0, quad < quads - 1)
    has_in = jnp.where(left, quad < quads - 1, quad > 0)
    side_in = jnp.where(left, 1, 0)
    side_out = 1 - side_in
    twin = jnp.where(gate, d - s, d + s)
    across_to = jnp.where(gate, d + s, d + 3 * s)
    hosts = outer & has_in
    guests = outer & has_out
    gets_skew = gate & has_out

    fars = []
    for distance in (4, 8):
        fars.append((d + distance, d + distance < n_ctx))
        fars.append((d - distance, d - distance >= 0))
    arrives = [fars[1], fars[0], fars[3], fars[2]]
    far_rows = (cap2 * bs, cap2 * bs, cap3 * bs, cap3 * bs)
    far_start = (0, cap2 * bs, 2 * cap2 * bs, (2 * cap2 + cap3) * bs)
    far_blocks = [pl.ds(a // bs, n // bs) for a, n in zip(far_start, far_rows)]
    hosted = (outer & left, outer & jnp.logical_not(left), jnp.bool_(False), jnp.bool_(False))
    far_sends = [ok & jnp.logical_not(hosted[i]) for i, (_, ok) in enumerate(fars)]
    far_gets = [ok & jnp.logical_not(hosted[i]) for i, (_, ok) in enumerate(arrives)]
    guest_slot = jnp.where(left, 0, 1)

    def to(device):
        return {"ctx": device}

    barrier = pltpu.get_barrier_semaphore()
    always = jnp.bool_(True)
    partners = [(p, ok) for p, ok in fars]
    partners += [
        (twin, always),
        (across_to, always),
        (d + 5 * s, hosts),
        (d - 5 * s, gets_skew),
    ]
    count = jnp.int32(0)
    for p, ok in partners:
        count = count + ok.astype(jnp.int32)

        @pl.when(ok)
        def _(p=p):
            pl.semaphore_signal(barrier, inc=1, device_id=to(p), device_id_type=MESH)

    pl.semaphore_wait(barrier, count)

    def remote(src, dst, ssem, rsem, device):
        return pltpu.make_async_remote_copy(
            src_ref=src, dst_ref=dst, send_sem=ssem, recv_sem=rsem,
            device_id=to(device), device_id_type=MESH,
        )

    def span(c):
        return pl.ds(pl.multiple_of(c * cols_piece, cols_piece), cols_piece)

    flip = (1, 0, 3, 2)

    def list_copy(slot, device):
        return remote(lists.at[0], lists_got.at[slot], s_list.at[slot], r_list.at[slot], device)

    def count_copy():
        return remote(counts, counts_got, s_count, r_count, d - 4 * s)

    def near_copy(kv):
        return remote((k_hbm, v_hbm)[kv], near.at[kv], s_near.at[kv], r_near.at[kv], twin)

    def across_copy(c, kv):
        x = span(c)
        return remote(
            (k_hbm, v_hbm)[kv].at[:, :, x], across.at[kv, :, :, x], s_across, r_across.at[kv, c], across_to
        )

    def passed_copy(c):
        x = span(c)
        return remote(across.at[:, :, :, x], passed.at[:, :, :, x], s_passed, r_passed.at[c], twin)

    def skew_copy(c):
        x = span(c)
        return remote(skew_pack.at[:, :, :, x], skew.at[:, :, :, x], s_skew, r_skew.at[c], d + 5 * s)

    def far_copy(i, c):
        r, x = far_blocks[i], span(c)
        return remote(
            far_pack.at[:, r, :, x], far.at[:, r, :, x], s_far.at[i], r_far.at[i, c], fars[i][0]
        )

    def q_copy(c):
        x = span(c)
        return remote(q_hbm.at[:, x], q_got.at[:, x], s_q, r_q.at[c], d - 4 * s)

    def o_copy(c):
        x = span(c)
        return remote(o_send.at[:, x], o_got.at[:, x], s_o, r_o.at[c], d + 4 * s)

    def lse_copy(c):
        h = pl.ds(c * piece, piece)
        return remote(lse_send.at[h], lse_got.at[h], s_lse, r_lse.at[c], d + 4 * s)

    def each_piece(one):
        def step(c, carry):
            one(c)
            return carry

        lax.fori_loop(0, pieces, step, 0)

    list_sends = [(flip[i], p, ok) for i, (p, ok) in enumerate(fars)] + [(4, d - 5 * s, gets_skew)]
    list_gets = [(i, p, ok) for i, (p, ok) in enumerate(fars)] + [(4, d + 5 * s, hosts)]
    for slot, p, ok in list_sends:
        @pl.when(ok)
        def _(slot=slot, p=p):
            list_copy(slot, p).start()

    @pl.when(guests)
    def _():
        count_copy().start()

    def start_across(c):
        for kv in range(2):
            across_copy(c, kv).start()

    each_piece(start_across)
    for kv in range(2):
        near_copy(kv).start()

    for i in range(4):
        @pl.when(jnp.logical_not(far_gets[i]))
        def _(i=i):
            for kv in range(2):
                far[kv, far_blocks[i]] = jnp.zeros((far_rows[i] // bs, bs, width), far.dtype)

    spare = far_room - sum(far_rows)
    if spare:
        for kv in range(2):
            far[kv, pl.ds(sum(far_rows) // bs, spare // bs)] = jnp.zeros(
                (spare // bs, bs, width), far.dtype
            )

    @pl.when(gate & jnp.logical_not(has_out))
    def _():
        for kv in range(2):
            skew[kv] = jnp.zeros(skew.shape[1:], skew.dtype)

    @pl.when(outer & jnp.logical_not(has_out))
    def _():
        o_got[...] = jnp.zeros(o_got.shape, o_got.dtype)
        lse_got[...] = jnp.full(lse_got.shape, MASKED, lse_got.dtype)

    for copy in own:
        copy.wait()

    def flat(x):
        return x.reshape(x.shape[0] * x.shape[1], x.shape[2])

    for i, p, ok in list_gets:
        @pl.when(ok)
        def _(i=i, p=p):
            list_copy(i, p).wait_recv()
            if i < 4:
                for j in range(far_rows[i] // bs):
                    source = lists_got[i, 2 + i // 2, i % 2, j]
                    far_pack[0, far_start[i] // bs + j] = k_ref[source]
                    far_pack[1, far_start[i] // bs + j] = v_ref[source]

    @pl.when(hosts)
    def _():
        count_copy().wait_recv()

    def start_far(c):
        @pl.when(guests)
        def _():
            q_copy(c).start()

        for i in range(4):
            @pl.when(far_sends[i])
            def _(i=i):
                far_copy(i, c).start()

    each_piece(start_far)

    def as_bias(seen):
        return jnp.where(seen, 0.0, MASKED).astype(jnp.float32)

    def full_bias(listed, counted):
        block = lax.broadcasted_iota(jnp.int32, (1, rows), 1) // bs
        seen = jnp.zeros((1, rows), jnp.int32)
        for j in range(nblk):
            hit = (block == listed(j)) & (jnp.full((1, rows), j) < counted)
            seen = seen + hit.astype(jnp.int32)
        return as_bias(seen > 0)

    def listed_bias(n, counted):
        column = lax.broadcasted_iota(jnp.int32, (1, n), 1)
        return as_bias(column < counted * bs)

    half = cap1 * bs
    quarter = cap2 * bs
    side_near = jnp.where(gate, side_out, side_in)
    bias_near[...] = full_bias(lambda j: lists[0, 0, side_near, j], counts[0, side_near, 0])
    column = lax.broadcasted_iota(jnp.int32, (1, far_room), 1)
    limit = jnp.zeros(column.shape, jnp.int32)
    for i in range(4):
        shown = jnp.where(far_gets[i], counts[0, i % 2, 2 + i // 2], 0)
        limit = jnp.where(column >= far_start[i], far_start[i] + shown * bs, limit)
    limit = jnp.where(column >= sum(far_rows), 0, limit)
    bias_late[:, :far_room] = as_bias(column < limit)
    bias_late[:, far_room:far_room + half] = listed_bias(half, counts[0, side_in, 1])
    bias_late[:, far_room + half:far_room + 2 * half] = listed_bias(half, counts[0, side_out, 1])
    bias_late[:, far_room + 2 * half:] = full_bias(
        lambda j: lists[0, 0, side_in, j], counts[0, side_in, 0]
    )

    @pl.when(hosts)
    def _():
        bias_guest[:, :rows] = full_bias(
            lambda j: lists_got[guest_slot, 0, side_out, j], counts_got[0, side_out, 0]
        )
        bias_guest[:, rows:rows + half] = listed_bias(half, counts_got[0, side_out, 1])
        bias_guest[:, rows + half:] = listed_bias(
            bias_guest.shape[1] - rows - half, counts_got[0, side_out, 2]
        )

    def wide(x, n):
        return jnp.concatenate([x] * (n // HEAD), axis=1)

    def folded(p):
        total = p[:, :HEAD]
        for i in range(1, p.shape[1] // HEAD):
            total = total + p[:, i * HEAD:(i + 1) * HEAD]
        return total

    def scores(q, k):
        return lax.dot_general(
            q, k, (((1,), (1,)), ((), ())), preferred_element_type=jnp.float32
        ) * rate

    def weigh(sc, v, old=None):
        n = sc.shape[1]
        best = jnp.broadcast_to(jnp.max(sc, axis=1, keepdims=True), (rows, HEAD))
        if old is not None:
            best = jnp.maximum(old, best)
        p = jnp.exp2(sc - wide(best, n))
        mixed = jnp.dot(p.astype(jnp.bfloat16), v, preferred_element_type=jnp.float32)
        return best, folded(p), mixed

    def head_cols(h):
        return pl.ds(pl.multiple_of(h * HEAD, HEAD), HEAD)

    together = max(n for n in (1, 2, 3, 4, 5) if heads % n == 0)

    for kv in range(2):
        near_copy(kv).wait_recv()

    def early(h):
        x = head_cols(h)
        q = q_ref[:, x]
        sc = jnp.concatenate(
            [scores(q, flat(k_ref[:, :, x])), scores(q, flat(near[0, :, :, x])) + bias_near[...]], axis=1
        )
        top[h], tot[h], acc[h] = weigh(
            sc, jnp.concatenate([flat(v_ref[:, :, x]), flat(near[1, :, :, x])], axis=0)
        )

    def early_step(i, carry):
        for u in range(together):
            early(together * i + u)
        return carry

    lax.fori_loop(0, heads // together, early_step, 0)

    def listed(kv, level, side, n, x, of):
        return jnp.concatenate(
            [stage[kv, of(level, side, j), :, x] for j in range(n)], axis=0
        )

    def mine(level, side, j):
        return lists[0, level, side, j]

    def theirs(level, side, j):
        return lists_got[guest_slot, level, side, j]

    def wait_far(c):
        for i in range(4):
            @pl.when(far_gets[i])
            def _(i=i):
                far_copy(i, c).wait_recv()

    def late(h, u, n_bias, extra):
        x = head_cols(h)
        y = pl.ds(u * HEAD, HEAD)
        k = [flat(far[0, :, :, x]), listed(0, 1, side_in, cap1, y, mine)]
        v = [flat(far[1, :, :, x]), listed(1, 1, side_in, cap1, y, mine)]
        if extra:
            k += [flat(skew[0, :, :, x]), flat(across[0, :, :, x])]
            v += [flat(skew[1, :, :, x]), flat(across[1, :, :, x])]
        sc = scores(q_ref[:, x], jnp.concatenate(k, axis=0)) + bias_late[:, :n_bias]
        old = top[h]
        best, total, mixed = weigh(sc, jnp.concatenate(v, axis=0), old)
        factor = jnp.exp2(old - best)
        return best, tot[h] * factor + total, acc[h] * factor + mixed

    def gate_piece(c):
        passed_copy(c).wait_recv()
        wait_far(c)

        @pl.when(has_out)
        def _():
            skew_copy(c).wait_recv()

        stage[...] = passed[:, :, :, span(c)]
        for u in range(piece):
            h = c * piece + u
            _, total, mixed = late(h, u, bias_late.shape[1], True)
            total = jnp.sum(total, axis=1, keepdims=True)
            out_ref[:, head_cols(h)] = (mixed / total).astype(out_ref.dtype)

    def send_skew(c):
        x = span(c)
        stage[...] = across[:, :, :, x]
        for kv in range(2):
            for j in range(cap1):
                skew_pack[kv, j, :, x] = stage[kv, lists_got[4, 1, side_out, j]]
        skew_copy(c).start()

    pad = bias_guest.shape[1] - rows - half - quarter

    def host(c):
        q_copy(c).wait_recv()
        for u in range(piece):
            h = c * piece + u
            x = head_cols(h)
            y = pl.ds(u * HEAD, HEAD)
            sides = []
            for kv, mine_ref in enumerate((k_ref, v_ref)):
                parts = [flat(across[kv, :, :, x]), listed(kv, 1, side_out, cap1, y, theirs)]
                parts += [mine_ref[theirs(2, side_out, j), :, x] for j in range(cap2)]
                if pad:
                    parts.append(jnp.zeros((pad, HEAD), across.dtype))
                sides.append(jnp.concatenate(parts, axis=0))
            sc = scores(q_got[:, x], sides[0]) + bias_guest[...]
            best, total, mixed = weigh(sc, sides[1])
            total = jnp.broadcast_to(jnp.sum(total, axis=1, keepdims=True), (rows, HEAD))
            o_send[:, x] = (mixed / total).astype(o_send.dtype)
            lse = best + jnp.log2(total)
            lse_send[h] = jnp.transpose(lse)[:8, :]
        o_copy(c).start()
        lse_copy(c).start()

    def outer_piece(c):
        @pl.when(has_in)
        def _():
            send_skew(c)

        passed_copy(c).wait_recv()
        stage[...] = passed[:, :, :, span(c)]

        @pl.when(has_in)
        def _():
            host(c)

        wait_far(c)
        for u in range(piece):
            h = c * piece + u
            top[h], tot[h], acc[h] = late(h, u, far_room + half, False)

    def outer_finish(c):
        @pl.when(has_out)
        def _():
            o_copy(c).wait_recv()
            lse_copy(c).wait_recv()

        for u in range(piece):
            h = c * piece + u
            x = head_cols(h)
            lse = jnp.transpose(jnp.broadcast_to(lse_got[h][:1, :], (HEAD, rows)))
            old = top[h]
            best = jnp.maximum(old, lse)
            factor, guest = jnp.exp2(old - best), jnp.exp2(lse - best)
            total = jnp.sum(tot[h], axis=1, keepdims=True) * factor + guest
            mixed = acc[h] * factor + o_got[:, x].astype(jnp.float32) * guest
            out_ref[:, x] = (mixed / total).astype(out_ref.dtype)

    def turn(c, carry):
        @pl.when(c < pieces)
        def _():
            for kv in range(2):
                across_copy(c, kv).wait_recv()
            passed_copy(c).start()

            @pl.when(outer)
            def _():
                outer_piece(c)

        @pl.when(c > 0)
        def _():
            @pl.when(gate)
            def _():
                gate_piece(c - 1)

            @pl.when(outer)
            def _():
                outer_finish(c - 1)

        return carry

    lax.fori_loop(0, pieces + 1, turn, 0)

    for slot, p, ok in list_sends:
        @pl.when(ok)
        def _(slot=slot, p=p):
            list_copy(slot, p).wait_send()

    for kv in range(2):
        near_copy(kv).wait_send()
    remote(across, across, s_across, r_across.at[0, 0], across_to).wait_send()
    remote(across, passed, s_passed, r_passed.at[0], twin).wait_send()
    for i in range(4):
        @pl.when(far_sends[i])
        def _(i=i):
            r = far_blocks[i]
            remote(
                far_pack.at[:, r], far.at[:, r], s_far.at[i], r_far.at[i, 0], fars[i][0]
            ).wait_send()

    @pl.when(guests)
    def _():
        count_copy().wait_send()
        remote(q_hbm, q_got, s_q, r_q.at[0], d - 4 * s).wait_send()

    @pl.when(hosts)
    def _():
        remote(skew_pack, skew, s_skew, r_skew.at[0], d + 5 * s).wait_send()
        remote(o_send, o_got, s_o, r_o.at[0], d + 4 * s).wait_send()
        remote(lse_send, lse_got, s_lse, r_lse.at[0], d + 4 * s).wait_send()


def shards(n_ctx, queries, keys, values, kv_lists, kv_counts):
    rows, width = queries.shape
    heads = width // HEAD
    nblk = kv_lists.shape[3]
    bs = rows // nblk
    half, quarter = nblk // 2 * bs, nblk // 4 * bs
    far_rows = 2 * (nblk // 4 + nblk // 8) * bs
    far_room = far_rows + (-far_rows) % HEAD
    guest_room = rows + half + quarter
    guest_room += (-guest_room) % HEAD
    piece = PIECE_HEADS if heads % PIECE_HEADS == 0 else 1
    pieces = heads // piece
    kv = jnp.bfloat16
    f32 = jnp.float32
    vmem = pl.BlockSpec(memory_space=pltpu.VMEM)
    hbm = pl.BlockSpec(memory_space=pl.ANY)
    smem = pl.BlockSpec(memory_space=pltpu.SMEM)
    dma = pltpu.SemaphoreType.DMA
    return pl.pallas_call(
        functools.partial(body, n_ctx, nblk, piece),
        out_shape=jax.ShapeDtypeStruct((rows, width), jnp.bfloat16),
        in_specs=[hbm, hbm, hbm, smem, smem],
        out_specs=vmem,
        scratch_shapes=[
            pltpu.VMEM((rows, width), kv),
            pltpu.VMEM((nblk, bs, width), kv),
            pltpu.VMEM((nblk, bs, width), kv),
            pltpu.VMEM((2, nblk, bs, width), kv),
            pltpu.VMEM((2, nblk, bs, width), kv),
            pltpu.VMEM((2, nblk, bs, width), kv),
            pltpu.VMEM((2, half // bs, bs, width), kv),
            pltpu.VMEM((2, half // bs, bs, width), kv),
            pltpu.VMEM((2, far_room // bs, bs, width), kv),
            pltpu.VMEM((2, far_rows // bs, bs, width), kv),
            pltpu.VMEM((2, nblk, bs, piece * HEAD), kv),
            pltpu.VMEM((rows, width), kv),
            pltpu.VMEM((rows, width), kv),
            pltpu.VMEM((rows, width), kv),
            pltpu.VMEM((heads, 8, rows), f32),
            pltpu.VMEM((heads, 8, rows), f32),
            pltpu.VMEM((heads, rows, HEAD), f32),
            pltpu.VMEM((heads, rows, HEAD), f32),
            pltpu.VMEM((heads, rows, HEAD), f32),
            pltpu.VMEM((1, rows), f32),
            pltpu.VMEM((1, far_room + 2 * half + rows), f32),
            pltpu.VMEM((1, guest_room), f32),
            pltpu.SMEM((5,) + kv_lists.shape[1:], jnp.int32),
            pltpu.SMEM((1, kv_counts.shape[2], kv_counts.shape[1]), jnp.int32),
            dma((5,)), dma, dma((2,)), dma, dma, dma, dma((4,)), dma, dma, dma,
            dma((3,)), dma((5,)), dma, dma((2,)), dma((2, pieces)), dma((pieces,)), dma((pieces,)),
            dma((4, pieces)), dma((pieces,)), dma((pieces,)), dma((pieces,)),
        ],
        compiler_params=pltpu.CompilerParams(
            collective_id=0, has_side_effects=True, vmem_limit_bytes=60 * 1024 * 1024
        ),
        name="radial",
    )(
        queries, keys.reshape(nblk, bs, width), values.reshape(nblk, bs, width),
        kv_lists, jnp.swapaxes(kv_counts, 1, 2),
    )


def solution(mesh):
    in_specs = (
        P(("groups", "ctx"), None),
        P(("groups", "ctx"), None),
        P(("groups", "ctx"), None),
        P("ctx", None, None, None),
        P("ctx", None, None),
    )
    out_specs = P(("groups", "ctx"), None)
    return jax.shard_map(
        functools.partial(shards, mesh.shape["ctx"]),
        mesh=mesh, in_specs=in_specs, out_specs=out_specs, check_vma=False,
    )
```

time: 84 us -> 72.6 us (0.86)
  the two profiles are of different devices: /device:TPU:17 before, /device:TPU:16 now
where the time goes in v1:
time: 72.6 us; the launch traced here: 72.5 us
  Pallas kernels  70 us (96%)
  local copies, waits for them, and re-layouts  2.46 us (3%)
    pallas_call x1, Pallas kernels, shards(): pl.pallas_call(functools.partial(body, n_ctx, nblk, piece), out_shape=jax...  70 us
    unnamed x1, local copies, waits for them, and re-layouts  2.46 us

profile of v1, /device:TPU:16, one launch (start us, length us, event | category | flops | bytes accessed | tf_op | source)
XLA Modules:
  0.0 72.5 jit_solution(8988768176088377476)
XLA Ops:
  0.0 70.0 %radial.1 = bf16[256,2560]{1,0:T(8,128)(2,1)} custom-call(bf16[256,2560]{1,0:T(8,128)(2,1)} %q_hbm.1, bf16[8,32,2560]{2,1,0:T(8,128)(2,1)} %bitcast.3, bf16[8,32,2560]{2,1,0:T(8,128)(2,1)} %bitcast.4, s32[1,4,2,8]{3,2,1,0:T(2,128)} %lists.1, s32[1,2,4]{2,1,0:T(2,128)} %bitcast.5), custom_call_target="tpu_custom_call" | custom-call | tf_op jit(solution)/shard_map/radial/pallas_call | solution.py:502
  70.0 2.5 %copy.7 = bf16[256,2560]{1,0:T(8,128)(2,1)} copy(bf16[256,2560]{1,0:T(8,128)(2,1)} %radial.1) | data formatting | bytes 2621440

commit v2 on v1

--- a/solution.py
+++ b/solution.py
@@ -501,7 +501,7 @@
     dma = pltpu.SemaphoreType.DMA
     return pl.pallas_call(
         functools.partial(body, n_ctx, nblk, piece),
-        out_shape=jax.ShapeDtypeStruct((rows, width), jnp.bfloat16),
+        out_shape=pltpu.VMEM((rows, width), jnp.bfloat16),
         in_specs=[hbm, hbm, hbm, smem, smem],
         out_specs=vmem,
         scratch_shapes=[

time: 72.6 us -> 70.2 us (0.967)
  local copies, waits for them, and re-layouts: 2.46 us -> 1.06 us
  Pallas kernels: 70 us -> 68.9 us
    unnamed x1, local copies, waits for them, and re-layouts: 2.46 us -> 1.06 us
    pallas_call x1, Pallas kernels: 70 us -> 68.9 us  [shards(): pl.pallas_call(functools.partial(body, n_ctx, nblk, piece), out_shape=plt...]
where the time goes in v2:
time: 70.2 us; the launch traced here: 70 us
  Pallas kernels  68.9 us (98%)
  local copies, waits for them, and re-layouts  1.06 us (2%)
    pallas_call x1, Pallas kernels, shards(): pl.pallas_call(functools.partial(body, n_ctx, nblk, piece), out_shape=plt...  68.9 us

profile of v2, /device:TPU:16, one launch (start us, length us, event | category | flops | bytes accessed | tf_op | source)
XLA Modules:
  0.0 70.0 jit_solution(10676899584975320456)
XLA Ops:
  0.0 68.9 %radial.1 = bf16[256,2560]{1,0:T(8,128)(2,1)S(1)} custom-call(bf16[256,2560]{1,0:T(8,128)(2,1)} %q_hbm.1, bf16[8,32,2560]{2,1,0:T(8,128)(2,1)} %bitcast.3, bf16[8,32,2560]{2,1,0:T(8,128)(2,1)} %bitcast.4, s32[1,4,2,8]{3,2,1,0:T(2,128)} %lists.1, s32[1,2,4]{2,1,0:T(2,128)} %bitcast.5), custom_call_target="tpu_custom_call" | custom-call | tf_op jit(solution)/shard_map/radial/pallas_call | solution.py:502
  68.9 1.1 %copy.7 = bf16[256,2560]{1,0:T(8,128)(2,1)} copy(bf16[256,2560]{1,0:T(8,128)(2,1)S(1)} %radial.1) | data formatting | bytes 2621440

commit v3 on v2

--- a/solution.py
+++ b/solution.py
@@ -10,7 +10,7 @@
 
 HEAD = 128
 MASKED = -1e30
-PIECE_HEADS = 2
+PIECE_HEADS = 1
 MESH = pl.DeviceIdType.MESH
 
 
@@ -20,7 +20,7 @@
     q_ref, k_ref, v_ref,
     near, across, passed, skew, skew_pack, far, far_pack, stage,
     q_got, o_send, o_got, lse_send, lse_got,
-    acc, top, tot, bias_near, bias_late, bias_guest, lists_got, counts_got,
+    acc, top, tot, bias_near, bias_late, bias_guest, lists_got, counts_got, ready,
     s_list, s_count, s_near, s_across, s_passed, s_skew, s_far, s_q, s_o, s_lse,
     r_own, r_list, r_count, r_near, r_across, r_passed, r_skew, r_far, r_q, r_o, r_lse,
 ):
@@ -75,7 +75,7 @@
 
     barrier = pltpu.get_barrier_semaphore()
     always = jnp.bool_(True)
-    partners = [(p, ok) for p, ok in fars]
+    partners = [(p, ok) for p, ok in fars[:2]]
     partners += [
         (twin, always),
         (across_to, always),
@@ -92,6 +92,13 @@
 
     pl.semaphore_wait(barrier, count)
 
+    @pl.when(fars[0][1] & fars[1][1])
+    def _():
+        for i in range(2):
+            pl.semaphore_signal(
+                ready.at[1 - i], inc=1, device_id=to(fars[i][0]), device_id_type=MESH
+            )
+
     def remote(src, dst, ssem, rsem, device):
         return pltpu.make_async_remote_copy(
             src_ref=src, dst_ref=dst, send_sem=ssem, recv_sem=rsem,
@@ -154,9 +161,10 @@
     list_sends = [(flip[i], p, ok) for i, (p, ok) in enumerate(fars)] + [(4, d - 5 * s, gets_skew)]
     list_gets = [(i, p, ok) for i, (p, ok) in enumerate(fars)] + [(4, d + 5 * s, hosts)]
     for slot, p, ok in list_sends:
-        @pl.when(ok)
-        def _(slot=slot, p=p):
-            list_copy(slot, p).start()
+        if slot not in (2, 3):
+            @pl.when(ok)
+            def _(slot=slot, p=p):
+                list_copy(slot, p).start()
 
     @pl.when(guests)
     def _():
@@ -169,6 +177,12 @@
     each_piece(start_across)
     for kv in range(2):
         near_copy(kv).start()
+
+    for i in range(2):
+        @pl.when(fars[2 + i][1])
+        def _(i=i):
+            pl.semaphore_wait(ready.at[i], 1)
+            list_copy(flip[2 + i], fars[2 + i][0]).start()
 
     for i in range(4):
         @pl.when(jnp.logical_not(far_gets[i]))
@@ -529,6 +543,7 @@
             pltpu.VMEM((1, guest_room), f32),
             pltpu.SMEM((5,) + kv_lists.shape[1:], jnp.int32),
             pltpu.SMEM((1, kv_counts.shape[2], kv_counts.shape[1]), jnp.int32),
+            pltpu.SemaphoreType.REGULAR((2,)),
             dma((5,)), dma, dma((2,)), dma, dma, dma, dma((4,)), dma, dma, dma,
             dma((3,)), dma((5,)), dma, dma((2,)), dma((2, pieces)), dma((pieces,)), dma((pieces,)),
             dma((4, pieces)), dma((pieces,)), dma((pieces,)), dma((pieces,)),

time: 70.2 us -> 69 us (0.983)
  Pallas kernels: 68.9 us -> 67.3 us
    pallas_call x1, Pallas kernels: 68.9 us -> 67.3 us  [shards(): pl.pallas_call(functools.partial(body, n_ctx, nblk, piece), out_shape=plt...]
where the time goes in v3:
time: 69 us; the launch traced here: 68.3 us
  Pallas kernels  67.3 us (98%)
  local copies, waits for them, and re-layouts  1.06 us (2%)
    pallas_call x1, Pallas kernels, shards(): pl.pallas_call(functools.partial(body, n_ctx, nblk, piece), out_shape=plt...  67.3 us

profile of v3, /device:TPU:16, one launch (start us, length us, event | category | flops | bytes accessed | tf_op | source)
XLA Modules:
  0.0 68.3 jit_solution(14301921334656220666)
XLA Ops:
  0.0 67.3 %radial.1 = bf16[256,2560]{1,0:T(8,128)(2,1)S(1)} custom-call(bf16[256,2560]{1,0:T(8,128)(2,1)} %q_hbm.1, bf16[8,32,2560]{2,1,0:T(8,128)(2,1)} %bitcast.3, bf16[8,32,2560]{2,1,0:T(8,128)(2,1)} %bitcast.4, s32[1,4,2,8]{3,2,1,0:T(2,128)} %lists.1, s32[1,2,4]{2,1,0:T(2,128)} %bitcast.5), custom_call_target="tpu_custom_call" | custom-call | tf_op jit(solution)/shard_map/radial/pallas_call | solution.py:516
  67.3 1.1 %copy.7 = bf16[256,2560]{1,0:T(8,128)(2,1)} copy(bf16[256,2560]{1,0:T(8,128)(2,1)S(1)} %radial.1) | data formatting | bytes 2621440

commit v4 on v3

--- a/solution.py
+++ b/solution.py
@@ -10,7 +10,9 @@
 
 HEAD = 128
 MASKED = -1e30
-PIECE_HEADS = 1
+PIECE_HEADS = 2
+DETOUR = 1
+FORWARD_AT = 1
 MESH = pl.DeviceIdType.MESH
 
 
@@ -18,11 +20,11 @@
     n_ctx, nblk, piece,
     q_hbm, k_hbm, v_hbm, lists, counts, out_ref,
     q_ref, k_ref, v_ref,
-    near, across, passed, skew, skew_pack, far, far_pack, stage,
+    near, across, passed, relay, edge_pack, skew, skew_pack, far, far_pack, stage,
     q_got, o_send, o_got, lse_send, lse_got,
     acc, top, tot, bias_near, bias_late, bias_guest, lists_got, counts_got, ready,
-    s_list, s_count, s_near, s_across, s_passed, s_skew, s_far, s_q, s_o, s_lse,
-    r_own, r_list, r_count, r_near, r_across, r_passed, r_skew, r_far, r_q, r_o, r_lse,
+    s_list, s_count, s_near, s_across, s_relay, s_passed, s_skew, s_far, s_q, s_o, s_lse,
+    r_own, r_list, r_count, r_near, r_across, r_relay, r_passed, r_skew, r_far, r_q, r_o, r_lse,
 ):
     own = [
         pltpu.make_async_copy(src, dst, r_own.at[i])
@@ -56,6 +58,17 @@
     hosts = outer & has_in
     guests = outer & has_out
     gets_skew = gate & has_out
+    edge = outer & jnp.logical_not(has_out)
+    gets_edge = outer & jnp.logical_not(has_in)
+    asks_edge = gate & jnp.logical_not(has_in)
+    detours = gate & has_out
+    most = relay.shape[3] // cols_piece
+    n_detour = jnp.where(
+        detours, jnp.minimum(DETOUR * jnp.where(left, quads - quad, quad + 1), most), 0
+    )
+    n_relay = jnp.where(
+        detours, jnp.minimum(DETOUR * jnp.where(left, quad, quads - 1 - quad), most), 0
+    )
 
     fars = []
     for distance in (4, 8):
@@ -81,6 +94,8 @@
         (across_to, always),
         (d + 5 * s, hosts),
         (d - 5 * s, gets_skew),
+        (d - 3 * s, detours),
+        (d + 2 * s, edge | asks_edge),
     ]
     count = jnp.int32(0)
     for p, ok in partners:
@@ -125,6 +140,30 @@
             (k_hbm, v_hbm)[kv].at[:, :, x], across.at[kv, :, :, x], s_across, r_across.at[kv, c], across_to
         )
 
+    def edge_copy(c, kv):
+        x = span(c)
+        return remote(
+            edge_pack.at[kv, :, :, x], across.at[kv, pl.ds(0, cap1), :, x],
+            s_across, r_across.at[kv, c], across_to,
+        )
+
+    def detour_copy(i, kv):
+        return remote(
+            (k_hbm, v_hbm)[kv].at[:, :, span(pieces - n_detour + i)],
+            relay.at[kv, :, :, span(i)], s_across, r_relay.at[kv, i], d - 3 * s,
+        )
+
+    def detour_wait(i, kv):
+        x = relay.at[kv, :, :, span(i)]
+        remote(x, x, s_across, r_relay.at[kv, i], d - 3 * s).wait_recv()
+
+    def relay_copy(i, kv):
+        c = pieces - n_relay + i
+        return remote(
+            relay.at[kv, :, :, span(i)], across.at[kv, :, :, span(c)],
+            s_relay.at[kv, i], r_across.at[kv, c], d - 4 * s,
+        )
+
     def passed_copy(c):
         x = span(c)
         return remote(across.at[:, :, :, x], passed.at[:, :, :, x], s_passed, r_passed.at[c], twin)
@@ -143,23 +182,26 @@
         x = span(c)
         return remote(q_hbm.at[:, x], q_got.at[:, x], s_q, r_q.at[c], d - 4 * s)
 
-    def o_copy(c):
-        x = span(c)
-        return remote(o_send.at[:, x], o_got.at[:, x], s_o, r_o.at[c], d + 4 * s)
-
-    def lse_copy(c):
-        h = pl.ds(c * piece, piece)
-        return remote(lse_send.at[h], lse_got.at[h], s_lse, r_lse.at[c], d + 4 * s)
-
-    def each_piece(one):
+    def o_copy(h):
+        x = head_cols(h)
+        return remote(o_send.at[:, x], o_got.at[:, x], s_o, r_o.at[h], d + 4 * s)
+
+    def lse_copy(h):
+        return remote(lse_send.at[h], lse_got.at[h], s_lse, r_lse.at[h], d + 4 * s)
+
+    def each_piece(one, n=pieces):
         def step(c, carry):
             one(c)
             return carry
 
-        lax.fori_loop(0, pieces, step, 0)
-
-    list_sends = [(flip[i], p, ok) for i, (p, ok) in enumerate(fars)] + [(4, d - 5 * s, gets_skew)]
-    list_gets = [(i, p, ok) for i, (p, ok) in enumerate(fars)] + [(4, d + 5 * s, hosts)]
+        lax.fori_loop(0, n, step, 0)
+
+    list_sends = [(flip[i], p, ok) for i, (p, ok) in enumerate(fars)] + [
+        (4, d - 5 * s, gets_skew), (5, d + 2 * s, asks_edge)
+    ]
+    list_gets = [(i, p, ok) for i, (p, ok) in enumerate(fars)] + [
+        (4, d + 5 * s, hosts), (5, d + 2 * s, edge)
+    ]
     for slot, p, ok in list_sends:
         if slot not in (2, 3):
             @pl.when(ok)
@@ -170,11 +212,16 @@
     def _():
         count_copy().start()
 
+    def start_detour(i):
+        for kv in range(2):
+            detour_copy(i, kv).start()
+
     def start_across(c):
         for kv in range(2):
             across_copy(c, kv).start()
 
-    each_piece(start_across)
+    each_piece(start_detour, n_detour)
+    each_piece(start_across, jnp.where(edge, 0, pieces - n_detour))
     for kv in range(2):
         near_copy(kv).start()
 
@@ -222,6 +269,19 @@
                     source = lists_got[i, 2 + i // 2, i % 2, j]
                     far_pack[0, far_start[i] // bs + j] = k_ref[source]
                     far_pack[1, far_start[i] // bs + j] = v_ref[source]
+
+    @pl.when(edge)
+    def _():
+        for j in range(cap1):
+            source = lists_got[5, 1, side_out, j]
+            edge_pack[0, j] = k_ref[source]
+            edge_pack[1, j] = v_ref[source]
+
+        def start_edge(c):
+            for kv in range(2):
+                edge_copy(c, kv).start()
+
+        each_piece(start_edge)
 
     @pl.when(hosts)
     def _():
@@ -335,7 +395,7 @@
         )
 
     def mine(level, side, j):
-        return lists[0, level, side, j]
+        return jnp.where(asks_edge, j, lists[0, level, side, j])
 
     def theirs(level, side, j):
         return lists_got[guest_slot, level, side, j]
@@ -404,8 +464,8 @@
             o_send[:, x] = (mixed / total).astype(o_send.dtype)
             lse = best + jnp.log2(total)
             lse_send[h] = jnp.transpose(lse)[:8, :]
-        o_copy(c).start()
-        lse_copy(c).start()
+            o_copy(h).start()
+            lse_copy(h).start()
 
     def outer_piece(c):
         @pl.when(has_in)
@@ -425,13 +485,14 @@
             top[h], tot[h], acc[h] = late(h, u, far_room + half, False)
 
     def outer_finish(c):
-        @pl.when(has_out)
-        def _():
-            o_copy(c).wait_recv()
-            lse_copy(c).wait_recv()
-
         for u in range(piece):
             h = c * piece + u
+
+            @pl.when(has_out)
+            def _(h=h):
+                o_copy(h).wait_recv()
+                lse_copy(h).wait_recv()
+
             x = head_cols(h)
             lse = jnp.transpose(jnp.broadcast_to(lse_got[h][:1, :], (HEAD, rows)))
             old = top[h]
@@ -445,8 +506,21 @@
         @pl.when(c < pieces)
         def _():
             for kv in range(2):
-                across_copy(c, kv).wait_recv()
+                @pl.when(gets_edge)
+                def _(kv=kv):
+                    edge_copy(c, kv).wait_recv()
+
+                @pl.when(jnp.logical_not(gets_edge))
+                def _(kv=kv):
+                    across_copy(c, kv).wait_recv()
+
             passed_copy(c).start()
+
+            @pl.when((c >= FORWARD_AT) & (c < FORWARD_AT + n_relay))
+            def _():
+                for kv in range(2):
+                    detour_wait(c - FORWARD_AT, kv)
+                    relay_copy(c - FORWARD_AT, kv).start()
 
             @pl.when(outer)
             def _():
@@ -473,7 +547,21 @@
 
     for kv in range(2):
         near_copy(kv).wait_send()
-    remote(across, across, s_across, r_across.at[0, 0], across_to).wait_send()
+    @pl.when(edge)
+    def _():
+        remote(
+            edge_pack, across.at[:, pl.ds(0, cap1)], s_across, r_across.at[0, 0], across_to
+        ).wait_send()
+
+    @pl.when(jnp.logical_not(edge))
+    def _():
+        remote(across, across, s_across, r_across.at[0, 0], across_to).wait_send()
+
+    def end_relay(i):
+        for kv in range(2):
+            relay_copy(i, kv).wait_send()
+
+    each_piece(end_relay, n_relay)
     remote(across, passed, s_passed, r_passed.at[0], twin).wait_send()
     for i in range(4):
         @pl.when(far_sends[i])
@@ -507,6 +595,7 @@
     guest_room += (-guest_room) % HEAD
     piece = PIECE_HEADS if heads % PIECE_HEADS == 0 else 1
     pieces = heads // piece
+    most = max(1, min(DETOUR * (n_ctx // 4 - 1), pieces // 3))
     kv = jnp.bfloat16
     f32 = jnp.float32
     vmem = pl.BlockSpec(memory_space=pltpu.VMEM)
@@ -525,6 +614,8 @@
             pltpu.VMEM((2, nblk, bs, width), kv),
             pltpu.VMEM((2, nblk, bs, width), kv),
             pltpu.VMEM((2, nblk, bs, width), kv),
+            pltpu.VMEM((2, nblk, bs, most * piece * HEAD), kv),
+            pltpu.VMEM((2, half // bs, bs, width), kv),
             pltpu.VMEM((2, half // bs, bs, width), kv),
             pltpu.VMEM((2, half // bs, bs, width), kv),
             pltpu.VMEM((2, far_room // bs, bs, width), kv),
@@ -541,12 +632,12 @@
             pltpu.VMEM((1, rows), f32),
             pltpu.VMEM((1, far_room + 2 * half + rows), f32),
             pltpu.VMEM((1, guest_room), f32),
-            pltpu.SMEM((5,) + kv_lists.shape[1:], jnp.int32),
+            pltpu.SMEM((6,) + kv_lists.shape[1:], jnp.int32),
             pltpu.SMEM((1, kv_counts.shape[2], kv_counts.shape[1]), jnp.int32),
             pltpu.SemaphoreType.REGULAR((2,)),
-            dma((5,)), dma, dma((2,)), dma, dma, dma, dma((4,)), dma, dma, dma,
-            dma((3,)), dma((5,)), dma, dma((2,)), dma((2, pieces)), dma((pieces,)), dma((pieces,)),
-            dma((4, pieces)), dma((pieces,)), dma((pieces,)), dma((pieces,)),
+            dma((6,)), dma, dma((2,)), dma, dma((2, most)), dma, dma, dma((4,)), dma, dma, dma,
+            dma((3,)), dma((6,)), dma, dma((2,)), dma((2, pieces)), dma((2, most)), dma((pieces,)), dma((pieces,)),
+            dma((4, pieces)), dma((pieces,)), dma((heads,)), dma((heads,)),
         ],
         compiler_params=pltpu.CompilerParams(
             collective_id=0, has_side_effects=True, vmem_limit_bytes=60 * 1024 * 1024

time: 69 us -> 67.9 us (0.984)
  Pallas kernels: 67.3 us -> 66.5 us
    pallas_call x1, Pallas kernels: 67.3 us -> 66.5 us  [shards(): pl.pallas_call(functools.partial(body, n_ctx, nblk, piece), out_shape=plt...]
where the time goes in v4:
time: 67.9 us; the launch traced here: 67.6 us
  Pallas kernels  66.5 us (98%)
  local copies, waits for them, and re-layouts  1.06 us (2%)
    pallas_call x1, Pallas kernels, shards(): pl.pallas_call(functools.partial(body, n_ctx, nblk, piece), out_shape=plt...  66.5 us

profile of v4, /device:TPU:16, one launch (start us, length us, event | category | flops | bytes accessed | tf_op | source)
XLA Modules:
  0.0 67.6 jit_solution(9617798907704631301)
XLA Ops:
  0.0 66.5 %radial.1 = bf16[256,2560]{1,0:T(8,128)(2,1)S(1)} custom-call(bf16[256,2560]{1,0:T(8,128)(2,1)} %q_hbm.1, bf16[8,32,2560]{2,1,0:T(8,128)(2,1)} %bitcast.3, bf16[8,32,2560]{2,1,0:T(8,128)(2,1)} %bitcast.4, s32[1,4,2,8]{3,2,1,0:T(2,128)} %lists.1, s32[1,2,4]{2,1,0:T(2,128)} %bitcast.5), custom_call_target="tpu_custom_call" | custom-call | tf_op jit(solution)/shard_map/radial/pallas_call | solution.py:605
  66.5 1.1 %copy.7 = bf16[256,2560]{1,0:T(8,128)(2,1)} copy(bf16[256,2560]{1,0:T(8,128)(2,1)S(1)} %radial.1) | data formatting | bytes 2621440
